TPU v7x, 32 devices: a whole 2x2x4 slice. The times are simulated.
32 devices in a mesh: groups: 2 (over y), row: 4 (over x, core), col: 4 (over z).
Axes of the slice: x: 2, y: 2, z: 4, core: 2. Of those that a mesh axis runs over, the one named last changes fastest.
Arguments:
- slope_matrix: bfloat16 [1024, 1024], P(('groups', 'row'), 'col'), parts along dimension 0, may hold values from -0.3125 to 0.3125
- prior_matrix: bfloat16 [1024, 1024], P(('groups', 'row'), 'col'), parts along dimension 0, may hold values from -0.3125 to 0.3125
- slope_blocks: int32 [8, 8], P(('groups', 'row'), 'col'), parts along dimension 0, may hold values from 0 to 23, as said below
- prior_blocks: int32 [8, 8], P(('groups', 'row'), 'col'), parts along dimension 0, may hold values from 0 to 23, as said below
- weight_ids: int32 [512], P(('groups', 'row')), parts along dimension 0, may hold values from 0 to 15
- valid_mask: int32 [512], P(('groups', 'row')), parts along dimension 0, may hold values 0 or 1
- noise_weights: float32 [32], P('groups'), parts along dimension 0, may hold values from 0.25 to 4
- prior_weights: bfloat16 [1024], P(('groups', 'row')), parts along dimension 0, may hold values from 0.19921875 to 2
- frames: float32 [6144, 64], P(('groups', 'row', 'col')), parts along dimension 0, may hold values from -6 to 6
Outputs:
- gram_matrix: float32 [6144, 3072], P(('groups', 'row'), 'col'), parts along dimension 0
- applied: float32 [6144, 64], P(('groups', 'row', 'col')), parts along dimension 0
There are 2 independent parts, one for each index of `groups`. A program takes and returns all parts, laid end to end along the dimension named above; each array names one. Nothing has to cross between parts.
Inputs may be any that keep to these rules, and one draw needn't show every extreme that they name: `slope_blocks`: row i names, for each block-column set c (entries c * 2 to c * 2 + 1), 2 distinct actuator blocks of that set, c * 6 to c * 6 + 5, in the order in which their blocks are stored. `prior_blocks`: row i names, for each block-column set c (entries c * 2 to c * 2 + 1), 2 distinct actuator blocks of that set, c * 6 to c * 6 + 5, in the order in which their blocks are stored.
All inputs are finite; a program needn't handle non-finite values. No bound on the sum of `valid_mask` on one device may be relied on, other than what follows from the above.
Results may differ from a plain program's by a relative error of at most 0.007.
Values may be sent and summed in bfloat16 or wider, within the bound.
No kernel may reach another device: no remote copies, remote signals or barrier semaphores. Data moves between devices by JAX's collectives and lax.ppermute only.
A program may use at most 128 MiB of HBM per device.

v0:
```python
import jax
import jax.numpy as jnp
from jax import lax
from jax.sharding import PartitionSpec as P

BS = 128
AB = 6


def from_root(block, axis, owner):
    block = jnp.where(lax.axis_index(axis) == owner, block, jnp.zeros_like(block))
    return lax.psum(block, axis)


def expand_blocks(values, block_ids, set_index):
    block_count = block_ids.shape[0]
    chosen = block_ids.shape[1]
    targets = set_index * AB + jnp.arange(AB, dtype=jnp.int32)
    onehot = (block_ids[:, :, None] == targets[None, None, :]).astype(jnp.bfloat16)
    shaped = values.reshape(block_count, BS, chosen, BS)
    expanded = jnp.einsum("rskb,rka->rsab", shaped, onehot, preferred_element_type=jnp.float32)
    return expanded.astype(jnp.bfloat16).reshape(block_count * BS, AB * BS)


def shards(
    slope_matrix,
    prior_matrix,
    slope_blocks,
    prior_blocks,
    weight_ids,
    valid_mask,
    noise_weights,
    prior_weights,
    frames,
):
    row_index = lax.axis_index("row")
    col_index = lax.axis_index("col")
    classes = jnp.arange(noise_weights.shape[0], dtype=jnp.int32)
    picked = jnp.sum(
        jnp.where(weight_ids[:, None] == classes[None, :], noise_weights[None, :], 0.0), axis=1
    )
    subap_weight = picked * valid_mask.astype(jnp.float32)
    slope_weight = jnp.repeat(subap_weight, 2).astype(jnp.bfloat16)
    local_rows = jnp.concatenate([slope_matrix, prior_matrix], axis=0)
    local_ids = jnp.concatenate([slope_blocks, prior_blocks], axis=0)
    local_weight = jnp.concatenate([slope_weight, prior_weights], axis=0)
    all_rows, all_ids, all_weight = (
        lax.all_gather(local_rows, "row", axis=0, tiled=True),
        lax.all_gather(local_ids, "row", axis=0, tiled=True),
        lax.all_gather(local_weight, "row", axis=0, tiled=True),
    )
    row_scale = all_weight.astype(jnp.float32)[:, None]
    weighted_rows = (all_rows.astype(jnp.float32) * row_scale).astype(jnp.bfloat16)
    weighted_cols = expand_blocks(weighted_rows, all_ids, col_index)
    sent_rows, sent_ids = (
        from_root(all_rows, "col", row_index),
        from_root(all_ids, "col", row_index),
    )
    row_dense = expand_blocks(sent_rows, sent_ids, row_index)
    gram_tile = lax.dot_general(
        row_dense, weighted_cols, (((0,), (0,)), ((), ())), preferred_element_type=jnp.float32
    )
    frames_rows = lax.all_gather(frames, "col", axis=0, tiled=True)
    frames_cols = from_root(frames_rows, "row", col_index)
    partial_image = jnp.dot(
        gram_tile, frames_cols, precision=lax.Precision.HIGHEST, preferred_element_type=jnp.float32
    )
    applied = lax.psum_scatter(partial_image, "col", scatter_dimension=0, tiled=True)
    return (gram_tile, applied)


def solution(mesh):
    in_specs = (
        P(("groups", "row"), "col"),
        P(("groups", "row"), "col"),
        P(("groups", "row"), "col"),
        P(("groups", "row"), "col"),
        P(("groups", "row")),
        P(("groups", "row")),
        P("groups"),
        P(("groups", "row")),
        P(("groups", "row", "col"), None),
    )
    out_specs = (P(("groups", "row"), "col"), P(("groups", "row", "col"), None))
    return jax.shard_map(shards, mesh=mesh, in_specs=in_specs, out_specs=out_specs, check_vma=False)
```

profile of v0, /device:TPU:0, one launch (start us, length us, event | category | flops | bytes accessed | tf_op | source)
XLA Modules:
  0.0 126.3 jit_solution(12584636910592303553)
XLA Ops:
  7.2 0.9 pad_maximum_fusion
  8.1 8.6 %all_gather.13 = bf16[1024,256]{1,0:T(8,128)(2,1)S(1)} all-gather(bf16[256,256]{1,0:T(8,128)(2,1)S(1)} %pad_maximum_fusion), channel_id=1, replica_groups=mesh['groups'=2,'row'=4,'col'=4] {'row'}, dimensions={0}, use_global_device_ids=true | all-gather | bytes 655360 | tf_op jit(solution)/shard_map/all_gather | solution.py:48
  16.8 0.9 reshape.31
  17.8 16.0 %all-gather.2 = f32[4,192,64]{1,2,0:T(8,128)S(1)} all-gather(f32[1,192,64]{1,2,0:T(8,128)S(1)} %bitcast.36), channel_id=1, replica_groups=mesh['groups'=2,'row'=4,'col'=4] {'col'}, dimensions={0}, use_global_device_ids=true | all-gather | bytes 245760 | tf_op jit(solution)/shard_map/all_gather | solution.py:63
  33.9 0.2 copy.31
  34.0 0.9 reshape.44
  35.0 5.1 %all-gather = s32[4,2,2]{2,1,0:T(2,128)S(1)} all-gather(s32[1,2,2]{2,1,0:T(2,128)S(1)} %add_bitcast_fusion), channel_id=1, replica_groups=mesh['groups'=2,'row'=4,'col'=4] {'row'}, dimensions={0}, use_global_device_ids=true | all-gather | bytes 80 | tf_op jit(solution)/shard_map/all_gather | solution.py:49
  40.1 0.1 copy.34
  40.2 7.8 %psum.21 = s32[8,2]{0,1:T(2,128)S(1)} all-reduce(s32[8,2]{0,1:T(2,128)S(1)} %broadcast_select_fusion.2), channel_id=1, replica_groups=mesh['groups'=2,'row'=4,'col'=4] {'col'}, use_global_device_ids=true, to_apply=%region_0.1 | all-reduce | flops 16 | bytes 128 | tf_op jit(solution)/shard_map/psum | solution.py:12
  47.9 0.1 copy.27
  48.1 0.1 select_reduce_fusion
  48.2 0.1 broadcast_in_dim.32
  48.2 0.2 convert_element_type.38
  48.4 5.1 %all-gather.1 = bf16[4,1,256]{2,1,0:T(2,128)(2,1)S(1)} all-gather(bf16[1,1,256]{2,1,0:T(2,128)(2,1)S(1)} %reshape.37), channel_id=1, replica_groups=mesh['groups'=2,'row'=4,'col'=4] {'row'}, dimensions={0}, use_global_device_ids=true | all-gather | bytes 2560 | tf_op jit(solution)/shard_map/all_gather | solution.py:50
  53.5 0.2 multiply_convert_fusion
  53.7 0.1 reshape.33
  53.8 2.2 %convolution_convert_fusion = bf16[8,6,128,128]{3,1,2,0:T(8,128)(2,1)} fusion(bf16[8,128,2,128]{3,2,1,0:T(2,128)(2,1)S(1)} %reshape.33, s32[6]{0:T(128)S(1)} %iota_add_fusion, s32[8,2]{1,0:T(8,128)S(1)} %bitcast.38), kind=kOutput, calls=%fused_computation | convolution fusion | flops 3932256 | bytes 2097240 | tf_op jit(solution)/shard_map/rskb,rka->rsab/dot_general | solution.py:21
  56.0 3.4 %all-reduce.3.cloned.1.call-done = bf16[8,128,2,128]{3,2,1,0:T(2,128)(2,1)} async-done(((bf16[8,128,2,128]{3,2,1,0:T(2,128)(2,1)}), bf16[8,128,2,128]{3,2,1,0:T(2,128)(2,1)}) %all-reduce.3.cloned.1.call-update) | async-done | bytes 524304 | tf_op jit(solution)/shard_map/psum | solution.py:12
  59.4 2.1 %convolution_convert_fusion.1 = bf16[8,6,128,128]{3,1,2,0:T(8,128)(2,1)S(1)} fusion(bf16[8,128,2,128]{3,2,1,0:T(2,128)(2,1)} %all-reduce.3.cloned.1.call-done, s32[6]{0:T(128)S(1)} %iota_add_fusion.1, s32[8,2]{1,0:T(8,128)S(1)} %copy.27), kind=kOutput, calls=%fused_computation.1 | convolution fusion | flops 3932256 | bytes 2097240 | tf_op jit(solution)/shard_map/rskb,rka->rsab/dot_general | solution.py:21
  61.5 1.5 %fusion = f32[768,768]{1,0:T(8,128)S(1)} fusion(bf16[128,8,6,128]{3,2,1,0:T(8,128)(2,1)S(1)} %bitcast.34, bf16[128,8,6,128]{3,2,1,0:T(8,128)(2,1)S(1)} %bitcast.35), kind=kOutput, calls=%fused_computation.2 | convolution fusion | flops 1207959552 | bytes 5505024 | tf_op jit(solution)/shard_map/dot_general | solution.py:60
  63.0 30.5 %all-reduce.5.cloned.1.call-done = f32[768,64]{0,1:T(8,128)} async-done(((f32[768,64]{0,1:T(8,128)}), f32[768,64]{0,1:T(8,128)}) %all-reduce.5.cloned.1.call-update) | async-done | bytes 196624 | tf_op jit(solution)/shard_map/psum | solution.py:12
  93.5 3.7 %fusion.13 = f32[768,64]{1,0:T(8,128)} fusion(f32[768,768]{1,0:T(8,128)S(1)} %fusion, f32[768,64]{0,1:T(8,128)} %all-reduce.5.cloned.1.call-done), kind=kOutput, calls=%fused_computation.27 | convolution fusion | flops 452984832 | bytes 2752512
  97.2 21.0 %reduce-scatter.4.cloned.1.call-done = f32[192,64]{1,0:T(8,128)} async-done(((f32[768,64]{1,0:T(8,128)}), f32[192,64]{1,0:T(8,128)}) %reduce-scatter.4.cloned.1.call-update) | async-done | bytes 49168
  118.2 1.6 %copy.38 = f32[192,64]{0,1:T(8,128)} copy(f32[192,64]{1,0:T(8,128)} %reduce-scatter.4.cloned.1.call-done) | data formatting | bytes 98304
  (34 shorter events, 0.3 us)
Async XLA Ops:
  7.2 10.7 %copy-start.2 = (f32[192,64]{0,1:T(8,128)S(1)}, f32[192,64]{0,1:T(8,128)}, u32[]{:S(2)}) copy-start(f32[192,64]{0,1:T(8,128)} %param.17) | copy-start | bytes 147460
  7.2 52.2 %all-reduce.3.cloned.1.call-start = ((), (), s32[]{:S(2)}) async-start(), calls=%async_computation.1 | async-start | bytes 1048576 | tf_op jit(solution)/shard_map/psum | solution.py:12
  16.8 18.2 %copy-start.3 = (s32[1,2]{1,0:T(1,128)S(1)}, s32[1,2]{1,0:T(1,128)}, u32[]{:S(2)}) copy-start(s32[1,2]{1,0:T(1,128)} %param.12) | copy-start | bytes 28
  16.8 18.2 %copy-start.4 = (s32[1,2]{1,0:T(1,128)S(1)}, s32[1,2]{1,0:T(1,128)}, u32[]{:S(2)}) copy-start(s32[1,2]{1,0:T(1,128)} %param.11) | copy-start | bytes 28
  16.8 31.3 %copy-start.5 = (f32[16]{0:T(128)S(1)}, f32[16]{0:T(128)}, u32[]{:S(2)}) copy-start(f32[16]{0:T(128)} %param.15) | copy-start | bytes 196
  16.8 31.3 %copy-start.6 = (s32[64]{0:T(128)S(1)}, s32[64]{0:T(128)}, u32[]{:S(2)}) copy-start(s32[64]{0:T(128)} %param.13) | copy-start | bytes 772
  16.8 31.4 %copy-start.7 = (s32[64]{0:T(128)S(1)}, s32[64]{0:T(128)}, u32[]{:S(2)}) copy-start(s32[64]{0:T(128)} %param.14) | copy-start | bytes 772
  16.8 31.6 %copy-start.8 = (bf16[128]{0:T(256)(128)(2,1)S(1)}, bf16[128]{0:T(256)(128)(2,1)}, u32[]{:S(2)}) copy-start(bf16[128]{0:T(256)(128)(2,1)} %param.16) | copy-start | bytes 772
  17.8 75.8 %all-reduce.5.cloned.1.call-start = ((), (), s32[]{:S(2)}) async-start(), calls=%async_computation.2 | async-start | bytes 393216 | tf_op jit(solution)/shard_map/psum | solution.py:12
  34.9 83.3 %reduce-scatter.4.cloned.1.call-start = ((), (), s32[]{:S(2)}) async-start(), calls=%async_computation.3 | async-start | bytes 491520
  59.4 2.1 %copy-start.1 = (bf16[8,6,128,128]{3,1,2,0:T(8,128)(2,1)S(1)}, bf16[8,6,128,128]{3,1,2,0:T(8,128)(2,1)}, u32[]{:S(2)}) copy-start(bf16[8,6,128,128]{3,1,2,0:T(8,128)(2,1)} %convolution_convert_fusion) | copy-start | bytes 4718596
  63.0 56.8 %copy-start = (f32[768,768]{1,0:T(8,128)}, f32[768,768]{1,0:T(8,128)S(1)}, u32[]{:S(2)}) copy-start(f32[768,768]{1,0:T(8,128)S(1)} %fusion) | copy-start | bytes 7077892
Sparse Core Ops, SparseCore 0:
  17.9 41.4 all-reduce.2
  61.7 31.7 all-reduce.4
  97.3 20.8 reduce-scatter.3
where the time goes:
time: 127 us; the launch traced here: 126 us
  waiting for transfers between devices  54.9 us (43%)
  blocking collectives  42.6 us (34%)
  between operations  13.9 us (11%)
  matrix products  9.43 us (7%)
  local copies, waits for them, and re-layouts  4.09 us (3%)
  other arithmetic  1.28 us (1%)
    psum x2, waiting for transfers between devices, from_root(): return lax.psum(block, axis)  33.9 us
    unnamed x4, waiting for transfers between devices  21 us
    all_gather x1, blocking collectives, shards(): frames_rows = lax.all_gather(frames, 'col', axis=0, tiled=True)  16 us
    all_gather x1, blocking collectives, shards(): lax.all_gather(local_rows, 'row', axis=0, tiled=True)  8.65 us
    psum x1, blocking collectives, from_root(): return lax.psum(block, axis)  7.79 us
    all_gather x1, blocking collectives, shards(): lax.all_gather(local_ids, 'row', axis=0, tiled=True)  5.07 us
    all_gather x1, blocking collectives, shards(): lax.all_gather(local_weight, 'row', axis=0, tiled=True)  5.07 us
    dot_general x2, matrix products, expand_blocks(): jnp.einsum('rskb,rka->rsab', shaped, onehot, preferred_element_type=jnp.f...  4.29 us
  transfers between devices with their start and end apart: 3, of which 3 were waited for; matrix products, arithmetic and copies ran while one was open for 6% of the time, Pallas kernels for 0%

commit v1 on v0

--- a/solution.py
+++ b/solution.py
@@ -7,9 +7,13 @@
 AB = 6
 
 
+def produce_wires(frame_in, device_axis):
+    return jnp.sum(lax.all_gather(frame_in, device_axis), axis=0)
+
+
 def from_root(block, axis, owner):
     block = jnp.where(lax.axis_index(axis) == owner, block, jnp.zeros_like(block))
-    return lax.psum(block, axis)
+    return produce_wires(block, axis)
 
 
 def expand_blocks(values, block_ids, set_index):

time: 127 us -> 105 us (0.83)
  waiting for transfers between devices: 54.9 us -> 20 us
  blocking collectives: 42.6 us -> 55 us
  other arithmetic: 1.28 us -> 4.73 us
  matrix products: 9.43 us -> 7.6 us
    psum x2 -> x0, waiting for transfers between devices: 33.9 us -> none  [from_root(): return lax.psum(block, axis)]
    all_gather x0 -> x2, blocking collectives: none -> 19.7 us  [produce_wires(): return jnp.sum(lax.all_gather(frame_in, device_axis), axis=0)]
    psum x1 -> x0, blocking collectives: 7.79 us -> none  [from_root(): return lax.psum(block, axis)]
    reduce_sum x0 -> x3, other arithmetic: none -> 2.65 us  [produce_wires(): return jnp.sum(lax.all_gather(frame_in, device_axis), axis=0)]
    unnamed x4 -> x3, waiting for transfers between devices: 21 us -> 19.7 us
  transfers between devices with their start and end apart: 3 -> 2, of which waited for: 3 -> 2; matrix products, arithmetic and copies ran while one was open for 6% -> 4% of each run, Pallas kernels for 0% -> 0%
where the time goes in v1:
time: 105 us
  blocking collectives  55 us (52%)
  waiting for transfers between devices  20 us (19%)
  between operations  14.3 us (14%)
  matrix products  7.6 us (7%)
  other arithmetic  4.73 us (5%)
  local copies, waits for them, and re-layouts  3.37 us (3%)
    all_gather x2, blocking collectives, produce_wires(): return jnp.sum(lax.all_gather(frame_in, device_axis), axis=0)  19.7 us
    unnamed x3, waiting for transfers between devices  19.7 us
    all_gather x1, blocking collectives, shards(): frames_rows = lax.all_gather(frames, 'col', axis=0, tiled=True)  16.3 us
    all_gather x1, blocking collectives, shards(): lax.all_gather(local_rows, 'row', axis=0, tiled=True)  8.78 us
    all_gather x1, blocking collectives, shards(): lax.all_gather(local_ids, 'row', axis=0, tiled=True)  5.07 us
    all_gather x1, blocking collectives, shards(): lax.all_gather(local_weight, 'row', axis=0, tiled=True)  5.07 us
    dot_general x2, matrix products, expand_blocks(): jnp.einsum('rskb,rka->rsab', shaped, onehot, preferred_element_type=jnp.f...  3.4 us
    unnamed x1, matrix products  2.72 us
  transfers between devices with their start and end apart: 2, of which 2 were waited for; matrix products, arithmetic and copies ran while one was open for 4% of the time, Pallas kernels for 0%

profile of v1, /device:TPU:0, one launch (start us, length us, event | category | flops | bytes accessed | tf_op | source)
XLA Modules:
  0.0 105.0 jit_solution(8541111687152717770)
XLA Ops:
  7.3 0.9 pad_maximum_fusion
  8.2 8.8 %all_gather.33 = bf16[1024,256]{1,0:T(8,128)(2,1)S(1)} all-gather(bf16[256,256]{1,0:T(8,128)(2,1)S(1)} %pad_maximum_fusion), channel_id=1, replica_groups=mesh['groups'=2,'row'=4,'col'=4] {'row'}, dimensions={0}, use_global_device_ids=true | all-gather | bytes 655360 | tf_op jit(solution)/shard_map/all_gather | solution.py:52
  17.0 0.8 broadcast_select_fusion
  17.9 5.1 %all-gather.3 = s32[4,2,2]{2,1,0:T(2,128)S(1)} all-gather(s32[1,2,2]{2,1,0:T(2,128)S(1)} %add_bitcast_fusion), channel_id=1, replica_groups=mesh['groups'=2,'row'=4,'col'=4] {'row'}, dimensions={0}, use_global_device_ids=true | all-gather | bytes 80 | tf_op jit(solution)/shard_map/all_gather | solution.py:53
  23.1 11.5 %all-gather.4 = s32[4,8,2]{1,2,0:T(2,128)S(1)} all-gather(s32[1,8,2]{1,2,0:T(2,128)S(1)} %select_bitcast_fusion), channel_id=2, replica_groups=mesh['groups'=2,'row'=4,'col'=4] {'col'}, dimensions={0}, use_global_device_ids=true | all-gather | bytes 320 | tf_op jit(solution)/shard_map/all_gather | solution.py:11
  34.8 0.2 convert_element_type.40
  35.0 5.1 %all-gather.5 = bf16[4,1,256]{2,1,0:T(2,128)(2,1)S(1)} all-gather(bf16[1,1,256]{2,1,0:T(2,128)(2,1)S(1)} %reshape.42), channel_id=1, replica_groups=mesh['groups'=2,'row'=4,'col'=4] {'row'}, dimensions={0}, use_global_device_ids=true | all-gather | bytes 2560 | tf_op jit(solution)/shard_map/all_gather | solution.py:54
  40.1 0.2 multiply_convert_fusion
  40.3 0.1 reshape.33
  40.4 16.3 %all-gather.6 = f32[4,192,64]{1,2,0:T(8,128)S(1)} all-gather(f32[1,192,64]{1,2,0:T(8,128)S(1)} %bitcast.42), channel_id=1, replica_groups=mesh['groups'=2,'row'=4,'col'=4] {'col'}, dimensions={0}, use_global_device_ids=true | all-gather | bytes 245760 | tf_op jit(solution)/shard_map/all_gather | solution.py:67
  56.8 0.2 copy.29
  56.9 0.2 reshape.49
  57.1 8.3 %all-gather.2 = f32[3072,64]{0,1:T(8,128)S(1)} all-gather(f32[768,64]{0,1:T(8,128)S(1)} %reshape.49), channel_id=4, replica_groups=mesh['groups'=2,'row'=4,'col'=4] {'row'}, dimensions={0}, use_global_device_ids=true | all-gather | bytes 983040 | tf_op jit(solution)/shard_map/all_gather | solution.py:11
  65.4 0.4 reshape.37
  65.8 0.5 reduce_sum.42
  66.3 2.2 %convolution_convert_fusion = bf16[8,6,128,128]{3,1,2,0:T(8,128)(2,1)} fusion(bf16[8,128,2,128]{3,2,1,0:T(2,128)(2,1)S(1)} %reshape.33, s32[6]{0:T(128)S(1)} %iota_add_fusion, s32[8,2]{1,0:T(8,128)S(1)} %bitcast.44), kind=kOutput, calls=%fused_computation | convolution fusion | flops 3932256 | bytes 2097240 | tf_op jit(solution)/shard_map/rskb,rka->rsab/dot_general | solution.py:25
  68.5 0.2 all-gather.9.cloned.1.call-done
  68.7 2.2 %reduce_sum.40 = bf16[1024,256]{1,0:T(8,128)(2,1)S(1)} reduce(bf16[4,1024,256]{2,1,0:T(8,128)(2,1)} %bitcast.39, bf16[]{:T(256)} %constant.16.clone.1), dimensions={0}, to_apply=%region_1.2 | reduce | flops 786432 | bytes 2621442 | tf_op jit(solution)/shard_map/reduce_sum | solution.py:11
  71.0 1.2 %convolution_convert_fusion.1 = bf16[8,6,128,128]{3,1,2,0:T(8,128)(2,1)S(1)} fusion(bf16[8,128,2,128]{3,2,1,0:T(2,128)(2,1)S(1)} %reshape.31, s32[6]{0:T(128)S(1)} %iota_add_fusion.1, s32[8,2]{1,0:T(8,128)S(1)} %copy.25), kind=kOutput, calls=%fused_computation.1 | convolution fusion | flops 3932256 | bytes 2097240 | tf_op jit(solution)/shard_map/rskb,rka->rsab/dot_general | solution.py:25
  72.3 0.4 copy-done.1
  72.6 1.5 %fusion = f32[768,768]{1,0:T(8,128)S(1)} fusion(bf16[128,8,6,128]{3,2,1,0:T(8,128)(2,1)S(1)} %bitcast.40, bf16[128,8,6,128]{3,2,1,0:T(8,128)(2,1)S(1)} %bitcast.41), kind=kOutput, calls=%fused_computation.2 | convolution fusion | flops 1207959552 | bytes 5505024 | tf_op jit(solution)/shard_map/dot_general | solution.py:64
  74.1 2.7 %fusion.13 = f32[768,64]{1,0:T(8,128)} fusion(f32[768,768]{1,0:T(8,128)S(1)} %fusion, f32[768,64]{0,1:T(8,128)S(1)} %reduce_sum.42), kind=kOutput, calls=%fused_computation.27 | convolution fusion | flops 452984832 | bytes 2752512
  76.8 19.7 %reduce-scatter.4.cloned.1.call-done = f32[192,64]{1,0:T(8,128)} async-done(((f32[768,64]{1,0:T(8,128)}), f32[192,64]{1,0:T(8,128)}) %reduce-scatter.4.cloned.1.call-update) | async-done | bytes 49168
  96.6 1.6 %copy.36 = f32[192,64]{0,1:T(8,128)} copy(f32[192,64]{1,0:T(8,128)} %reduce-scatter.4.cloned.1.call-done) | data formatting | bytes 98304
  (36 shorter events, 0.7 us)
Async XLA Ops:
  7.2 10.7 %copy-start.4 = (s32[1,2]{1,0:T(1,128)S(1)}, s32[1,2]{1,0:T(1,128)}, u32[]{:S(2)}) copy-start(s32[1,2]{1,0:T(1,128)} %param.11) | copy-start | bytes 28
  7.2 10.7 %copy-start.3 = (s32[1,2]{1,0:T(1,128)S(1)}, s32[1,2]{1,0:T(1,128)}, u32[]{:S(2)}) copy-start(s32[1,2]{1,0:T(1,128)} %param.12) | copy-start | bytes 28
  7.2 27.4 %copy-start.6 = (s32[64]{0:T(128)S(1)}, s32[64]{0:T(128)}, u32[]{:S(2)}) copy-start(s32[64]{0:T(128)} %param.13) | copy-start | bytes 772
  7.2 27.4 %copy-start.5 = (f32[16]{0:T(128)S(1)}, f32[16]{0:T(128)}, u32[]{:S(2)}) copy-start(f32[16]{0:T(128)} %param.15) | copy-start | bytes 196
  7.2 27.5 %copy-start.7 = (s32[64]{0:T(128)S(1)}, s32[64]{0:T(128)}, u32[]{:S(2)}) copy-start(s32[64]{0:T(128)} %param.14) | copy-start | bytes 772
  7.2 27.7 %copy-start.8 = (bf16[128]{0:T(256)(128)(2,1)S(1)}, bf16[128]{0:T(256)(128)(2,1)}, u32[]{:S(2)}) copy-start(bf16[128]{0:T(256)(128)(2,1)} %param.16) | copy-start | bytes 772
  7.2 61.5 %all-gather.9.cloned.1.call-start = ((), (), s32[]{:S(2)}) async-start(), calls=%async_computation.1 | async-start | bytes 2621440 | tf_op jit(solution)/shard_map/all_gather | solution.py:11
  8.2 32.3 %copy-start.2 = (f32[192,64]{0,1:T(8,128)S(1)}, f32[192,64]{0,1:T(8,128)}, u32[]{:S(2)}) copy-start(f32[192,64]{0,1:T(8,128)} %param.17) | copy-start | bytes 147460
  17.8 78.7 %reduce-scatter.4.cloned.1.call-start = ((), (), s32[]{:S(2)}) async-start(), calls=%async_computation.2 | async-start | bytes 491520
  71.0 1.6 %copy-start.1 = (bf16[8,6,128,128]{3,1,2,0:T(8,128)(2,1)S(1)}, bf16[8,6,128,128]{3,1,2,0:T(8,128)(2,1)}, u32[]{:S(2)}) copy-start(bf16[8,6,128,128]{3,1,2,0:T(8,128)(2,1)} %convolution_convert_fusion) | copy-start | bytes 4718596
  74.1 24.1 %copy-start = (f32[768,768]{1,0:T(8,128)}, f32[768,768]{1,0:T(8,128)S(1)}, u32[]{:S(2)}) copy-start(f32[768,768]{1,0:T(8,128)S(1)} %fusion) | copy-start | bytes 7077892
Sparse Core Ops, SparseCore 0:
  17.9 50.7 all-gather.8
  77.0 19.5 reduce-scatter.3
